TPU v7x, 128 devices: a whole 4x4x4 slice. The times are simulated.
128 devices in a mesh: uv: 4 (over y), channel: 16 (over z, x_hi, core), parity: 2 (over x_lo).
Axes of the slice: x: 4 (x_hi: 2, x_lo: 2; x = x_hi * 2 + x_lo), y: 4, z: 4, core: 2. Of those that a mesh axis runs over, the one named last changes fastest.
Arguments:
- visibility: bfloat16 [2, 16, 128, 32, 128], P('parity', 'channel', 'uv'), may hold values from -6 to 6
- kernel: bfloat16 [2, 16, 128, 128, 256], P('parity', 'channel', 'uv'), may hold values from -0.5 to 0.5
- block_tile: int32 [2, 16, 128], P('parity', 'channel', 'uv'), may hold values from 0 to 255, as said below
- block_chan: int32 [2, 16, 128], P('parity', 'channel', 'uv'), may hold values from 0 to 48
- tile_owner: int32 [256], replicated, may hold values from 0 to 3, as said below
- inv_cov: bfloat16 [1024, 1024], replicated, as said below
Outputs:
- cross_power: float32 [1024, 65536], P(None, ('uv', 'channel', 'parity'))
- diff_power: float32 [1024, 65536], P(None, ('uv', 'channel', 'parity'))
Inputs may be any that keep to these rules, and one draw needn't show every extreme that they name: `tile_owner`: each owner index owns exactly 64 tiles. `block_tile`: call slot(t) // 4 the cell group of tile t. Among the 32 blocks of one device (one aligned run along the last dimension), at most 1 name tiles of the same owner and the same cell group. `inv_cov`: entries are finite.
All inputs are finite; a program needn't handle non-finite values.
Results may differ from a plain program's by a relative error of at most 0.0067.
Values may be sent and summed in bfloat16 or wider, within the bound.
No kernel may reach another device: no remote copies, remote signals or barrier semaphores. Data moves between devices by JAX's collectives and lax.ppermute only.
A program may use at most 128 MiB of HBM per device.

v0:
```python
import math

import jax
import jax.numpy as jnp
from jax import lax
from jax.sharding import PartitionSpec as P


def delay_table(count):
    indices = jnp.arange(count, dtype=jnp.int32)
    phase_int = indices[:, None] * indices[None, :] % count
    angles = phase_int.astype(jnp.float32) * (2.0 * math.pi / count)
    return jnp.concatenate([jnp.cos(angles), jnp.sin(angles)], axis=0).astype(jnp.bfloat16)


def accumulate(received, row_index, row_total):
    half_width = row_index.shape[1]
    pixels = received.shape[-1]
    values = jnp.moveaxis(received.reshape(-1, 2, half_width, pixels), 1, 0).reshape(2, -1, pixels)
    flat_rows = jnp.clip(row_index, 0, row_total - 1).reshape(-1).astype(jnp.int32)
    row_block = math.gcd(row_total, 512)

    def grid_block(block_index):
        targets = block_index * row_block + jnp.arange(row_block, dtype=jnp.int32)
        onehot = (targets[:, None] == flat_rows[None, :]).astype(jnp.bfloat16)
        summed = jnp.einsum("nm,rmp->rnp", onehot, values, preferred_element_type=jnp.float32)
        return summed.astype(jnp.bfloat16)

    pieces = lax.map(grid_block, jnp.arange(row_total // row_block, dtype=jnp.int32))
    return jnp.moveaxis(pieces, 1, 0).reshape(2, row_total, pixels)


def on_device(visibility, kernel, block_tile, block_chan, tile_owner, inv_cov):
    uv_count = lax.axis_size("uv")
    chan_count = lax.axis_size("channel")
    samples = visibility[0, 0]
    weights = kernel[0, 0]
    tile_ids = block_tile[0, 0]
    starts = block_chan[0, 0]
    blocks = samples.shape[0]
    doubled = samples.shape[1]
    half_width = doubled // 2
    pixels = weights.shape[2]
    channels = inv_cov.shape[0]
    chan_dev = channels // chan_count
    tile_total = tile_owner.shape[0]
    tile_dev = tile_total // uv_count
    group_tiles = tile_dev // chan_count
    dest_count = uv_count * chan_count
    slot_count = max(1, 2 * blocks // dest_count)
    slot_total = dest_count * slot_count
    partials = jnp.einsum(
        "bkv,bvp->bkp", samples, weights, preferred_element_type=jnp.float32
    ).astype(jnp.bfloat16)
    indices = jnp.arange(tile_total, dtype=jnp.int32)
    same_owner = (tile_owner[:, None] == tile_owner[None, :]) & (
        indices[:, None] < indices[None, :]
    )
    tile_slot = jnp.sum(same_owner.astype(jnp.int32), axis=0)
    picked = tile_ids[:, None] == indices[None, :]
    owner_of = jnp.sum(jnp.where(picked, tile_owner[None, :], 0), axis=1)
    slot_of = jnp.sum(jnp.where(picked, tile_slot[None, :], 0), axis=1)
    target = owner_of * chan_count + slot_of // group_tiles
    block_order = jnp.arange(blocks, dtype=jnp.int32)
    earlier = (target[:, None] == target[None, :]) & (block_order[:, None] < block_order[None, :])
    rank_of = jnp.sum(earlier.astype(jnp.int32), axis=0)
    position = target * slot_count + rank_of
    outgoing = jnp.zeros((slot_total, doubled, pixels), jnp.bfloat16).at[position].set(partials)
    out_slot = jnp.zeros((slot_total,), jnp.int32).at[position].set(slot_of)
    out_chan = (
        jnp.zeros((slot_total,), jnp.int32)
        .at[position]
        .set(starts + lax.axis_index("channel") * chan_dev)
    )
    chan_offsets = jnp.arange(half_width, dtype=jnp.int32)
    received, got_slot, got_chan = (
        lax.all_to_all(
            outgoing.reshape(uv_count, chan_count * slot_count, doubled, pixels),
            "uv",
            split_axis=0,
            concat_axis=0,
            tiled=True,
        ),
        lax.all_to_all(
            out_slot.reshape(uv_count, chan_count * slot_count),
            "uv",
            split_axis=0,
            concat_axis=0,
            tiled=True,
        ),
        lax.all_to_all(
            out_chan.reshape(uv_count, chan_count * slot_count),
            "uv",
            split_axis=0,
            concat_axis=0,
            tiled=True,
        ),
    )
    local_chan = got_chan.reshape(-1) - lax.axis_index("channel") * chan_dev
    row_index = (local_chan[:, None] + chan_offsets[None, :]) * tile_dev + got_slot.reshape(-1)[
        :, None
    ]
    owned_grid = accumulate(received, row_index, chan_dev * tile_dev)
    owned_grid = owned_grid.reshape(2, chan_dev, tile_dev * pixels)
    gridded = lax.all_to_all(owned_grid, "channel", split_axis=2, concat_axis=1, tiled=True)
    weighted = jnp.einsum(
        "ij,rjc->ric", inv_cov, gridded, preferred_element_type=jnp.float32
    ).astype(jnp.bfloat16)
    dft_table = delay_table(channels)
    projected = jnp.einsum("ij,rjc->ric", dft_table, weighted, preferred_element_type=jnp.float32)
    spec_real = projected[0, :channels] + projected[1, channels:]
    spec_imag = projected[1, :channels] - projected[0, channels:]
    spectra = jnp.stack([spec_real, spec_imag])[None]
    paired = lax.all_to_all(spectra, "parity", split_axis=3, concat_axis=0, tiled=True)
    even_half = paired[0]
    odd_half = paired[1]
    cross_power = (even_half[0] * odd_half[0] + even_half[1] * odd_half[1]) / channels
    differ = even_half - odd_half
    diff_power = (differ[0] * differ[0] + differ[1] * differ[1]) / channels
    return (cross_power, diff_power)


def solution(mesh):
    placed = (
        P("parity", "channel", "uv", None, None),
        P("parity", "channel", "uv", None, None),
        P("parity", "channel", "uv"),
        P("parity", "channel", "uv"),
        P(),
        P(),
    )
    return jax.shard_map(
        on_device,
        mesh=mesh,
        in_specs=placed,
        out_specs=(P(None, ("uv", "channel", "parity")), P(None, ("uv", "channel", "parity"))),
        check_vma=False,
    )
```

profile of v0, /device:TPU:1, one launch (start us, length us, event | category | flops | bytes accessed | tf_op | source)
XLA Modules:
  0.0 375.7 jit_solution(14375926572992085066)
XLA Ops:
  3.9 5.0 %all-to-all-start.1 = ((s32[4,1,16]{2,1,0:T(1,128)}), s32[4,1,16]{2,1,0:T(1,128)S(1)}, u32[]{:S(2)}, u32[]{:S(2)}) async-start(s32[4,1,16]{2,1,0:T(1,128)} %bitcast.13), calls=%async_computation.1 | async-start | bytes 4096 | tf_op jit(solution)/shard_map/all_to_all | solution.py:84
  13.1 4.2 %all-to-all-start = ((s32[4,1,16]{2,1,0:T(1,128)}), s32[4,1,16]{2,1,0:T(1,128)S(1)}, u32[]{:S(2)}, u32[]{:S(2)}) async-start(s32[4,1,16]{2,1,0:T(1,128)} %bitcast.12), calls=%async_computation | async-start | bytes 4096 | tf_op jit(solution)/shard_map/all_to_all | solution.py:91
  18.4 4.4 %scatter_fusion = bf16[64,32,256]{2,1,0:T(8,128)(2,1)} fusion(bf16[64,32,256]{2,1,0:T(8,128)(2,1)} %broadcast_in_dim.54, s32[32]{0:T(128)S(1)} %fusion.46, bf16[32,32,256]{2,1,0:T(8,128)(2,1)S(1)} %fusion.40), kind=kCustom, calls=%fused_computation.2 | custom fusion | bytes 1572992 | tf_op jit(solution)/shard_map/scatter | solution.py:68
  22.7 4.2 %all-to-all-start.2 = ((bf16[4,16,32,256]{3,2,1,0:T(8,128)(2,1)}), bf16[4,16,32,256]{3,2,1,0:T(8,128)(2,1)S(1)}, u32[]{:S(2)}, u32[]{:S(2)}) async-start(bf16[4,16,32,256]{3,2,1,0:T(8,128)(2,1)} %bitcast.7), calls=%async_computation.2 | async-start | bytes 2097152 | tf_op jit(solution)/shard_map/all_to_all | solution.py:77
  28.3 11.7 %all-to-all-done.2 = bf16[4,16,32,256]{3,2,1,0:T(8,128)(2,1)S(1)} async-done(((bf16[4,16,32,256]{3,2,1,0:T(8,128)(2,1)}), bf16[4,16,32,256]{3,2,1,0:T(8,128)(2,1)S(1)}, u32[]{:S(2)}, u32[]{:S(2)}) %all-to-all-start.2) | async-done | bytes 1048608 | tf_op jit(solution)/shard_map/all_to_all | solution.py:77
  41.1 33.6 %while.11 = (s32[]{:T(128)}, bf16[8,2,512,256]{3,2,1,0:T(8,128)(2,1)}, s32[8]{0:T(128)S(1)}, bf16[2,1024,256]{2,1,0:T(8,128)(2,1)}, s32[64]{0:T(128)S(1)}, /*index=5*/s32[64]{0:T(128)S(1)}, s32[]{:T(128)}, s32[1]{0:T(128)}) while((s32[]{:T(128)}, bf16[8,2,512,256]{3,2,1,0:T(8,128)(2,1)}, s32[8]{0:T(128)S(1)}, ...), condition=%wide.region_8.9_spmd.clone, body=%wide.region_7.8_spmd.clone.sunk | while | flops 537661952 | bytes 1593981 | solution.py:29
  51.0 2.8 fusion.60
  72.0 2.8 fusion.60
  74.8 4.5 %copy.38 = bf16[2,8,512,256]{3,2,1,0:T(8,128)(2,1)} copy(bf16[2,8,512,256]{3,2,0,1:T(8,128)(2,1)} %bitcast.106) | data formatting | bytes 8388608 | tf_op jit(solution)/shard_map/transpose | solution.py:30
  79.3 7.4 %reshape_reshape.3 = bf16[2,64,16384]{2,1,0:T(8,128)(2,1)} reshape(bf16[2,8,512,256]{3,2,1,0:T(8,128)(2,1)} %copy.38) | data formatting | bytes 8388608 | tf_op jit(solution)/shard_map/reshape;reshape | solution.py:104
  86.7 17.8 %copy.39 = bf16[2,64,16384]{1,0,2:T(2,128)(2,1)} copy(bf16[2,64,16384]{2,1,0:T(8,128)(2,1)} %reshape_reshape.3) | data formatting | bytes 8388608 | tf_op jit(solution)/shard_map/reshape;reshape | solution.py:104
  104.5 14.0 %reshape.226 = bf16[16,2,65536]{2,1,0:T(2,128)(2,1)} reshape(bf16[16384,2,64]{2,1,0:T(2,128)(2,1)} %bitcast.102) | data formatting | bytes 8388608
  118.5 10.7 %all-to-all-start.3 = ((bf16[16,2,65536]{2,1,0:T(2,128)(2,1)}), bf16[16,2,65536]{2,1,0:T(2,128)(2,1)}, u32[]{:S(2)}, u32[]{:S(2)}) async-start(bf16[16,2,65536]{2,1,0:T(2,128)(2,1)} %reshape.226), calls=%async_computation.3 | async-start | bytes 8388608 | tf_op jit(solution)/shard_map/all_to_all | solution.py:105
  129.2 17.7 %sine_convert_fusion = (bf16[1024,1024]{1,0:T(8,128)(2,1)}, bf16[1024,1024]{1,0:T(8,128)(2,1)}) fusion(), kind=kLoop, calls=%fused_computation.29 | loop fusion | flops 16777216 | bytes 4194304 | tf_op jit(solution)/shard_map/convert.1
  146.9 33.2 %all-to-all-done.3 = bf16[16,2,65536]{2,1,0:T(2,128)(2,1)} async-done(((bf16[16,2,65536]{2,1,0:T(2,128)(2,1)}), bf16[16,2,65536]{2,1,0:T(2,128)(2,1)}, u32[]{:S(2)}, u32[]{:S(2)}) %all-to-all-start.3) | async-done | bytes 4194336 | tf_op jit(solution)/shard_map/all_to_all | solution.py:105
  180.1 13.6 %reshape.227 = bf16[16384,2,64]{2,1,0:T(2,128)(2,1)} reshape(bf16[16,2,65536]{2,1,0:T(2,128)(2,1)} %all-to-all-done.3) | data formatting | bytes 8388608
  193.7 20.1 %copy.47 = bf16[2,64,16,1024]{3,1,2,0:T(8,128)(2,1)} copy(bf16[2,64,16,1024]{1,0,3,2:T(2,128)(2,1)} %bitcast.103) | data formatting | bytes 8388608 | tf_op jit(solution)/shard_map/all_to_all | solution.py:105
  213.8 22.7 %convolution_bitcast_fusion = f32[2,2048,1024]{1,2,0:T(8,128)} fusion(bf16[1024,1024]{1,0:T(8,128)(2,1)} %get-tuple-element.62, bf16[1024,1024]{1,0:T(8,128)(2,1)} %get-tuple-element.63, bf16[2,1024,1024]{2,1,0:T(8,128)(2,1)} %bitcast.105, bf16[1024,1024]{1,0:T(8,128)(2,1)S(1)} %copy-done), kind=kOutput, calls=%fused_computation.15 | convolution fusion | flops 12895387648 | bytes 27262976 | tf_op jit(solution)/shard_map/ij,rjc->ric/dot_general | solution.py:110
  236.6 10.3 %slice_add_fusion = (f32[1,1024,1024]{1,2,0:T(8,128)S(1)}, f32[1,1024,1024]{1,2,0:T(8,128)}) fusion(f32[2,2048,1024]{1,2,0:T(8,128)} %convolution_bitcast_fusion), kind=kLoop, calls=%fused_computation.24 | loop fusion | flops 2097152 | bytes 25165824 | tf_op jit(solution)/shard_map/add | solution.py:111
  246.8 3.0 maximum_bitcast_fusion
  249.9 7.9 %copy.43 = f32[1,2,1024,1024]{2,1,0,3:T(2,128)S(1)} copy(f32[1,2,1024,1024]{2,3,1,0:T(8,128)S(1)} %maximum_bitcast_fusion) | data formatting | bytes 16777216 | tf_op jit(solution)/shard_map/broadcast_in_dim | solution.py:113
  257.8 95.7 %all_to_all.56 = f32[1,2,1024,1024]{2,1,0,3:T(2,128)} all-to-all(f32[1,2,1024,1024]{2,1,0,3:T(2,128)S(1)} %copy.43), channel_id=1, replica_groups=mesh['uv'=4,'channel'=16,'parity'=2] {'parity'}, dimensions={3} | all-to-all | bytes 16777216 | tf_op jit(solution)/shard_map/all_to_all | solution.py:114
  353.5 13.2 %copy.44 = f32[1,2,1024,2,512]{4,2,1,0,3:T(8,128)} copy(f32[1,2,1024,2,512]{2,1,4,3,0:T(2,128)} %bitcast.104) | data formatting | bytes 16777216 | tf_op jit(solution)/shard_map/all_to_all | solution.py:114
  366.7 6.0 %fusion.31 = f32[1024,512]{1,0:T(8,128)} fusion(f32[2,1,2,1024,512]{4,3,2,1,0:T(8,128)} %bitcast.100), kind=kLoop, calls=%fused_computation.43 | loop fusion | flops 2097152 | bytes 10485760 | tf_op jit(solution)/shard_map/div | solution.py:117
  (68 shorter events, 36.6 us)
Async XLA Ops:
  0.6 213.2 %copy-start = (bf16[1024,1024]{1,0:T(8,128)(2,1)S(1)}, bf16[1024,1024]{1,0:T(8,128)(2,1)}, u32[]{:S(2)}) copy-start(bf16[1024,1024]{1,0:T(8,128)(2,1)} %param.13) | copy-start | bytes 6291460
  3.9 9.1 %all-to-all-start.1 = ((s32[4,1,16]{2,1,0:T(1,128)}), s32[4,1,16]{2,1,0:T(1,128)S(1)}, u32[]{:S(2)}, u32[]{:S(2)}) async-start(s32[4,1,16]{2,1,0:T(1,128)} %bitcast.13), calls=%async_computation.1 | async-start | bytes 4096 | tf_op jit(solution)/shard_map/all_to_all | solution.py:84
  13.1 9.7 %all-to-all-start = ((s32[4,1,16]{2,1,0:T(1,128)}), s32[4,1,16]{2,1,0:T(1,128)S(1)}, u32[]{:S(2)}, u32[]{:S(2)}) async-start(s32[4,1,16]{2,1,0:T(1,128)} %bitcast.12), calls=%async_computation | async-start | bytes 4096 | tf_op jit(solution)/shard_map/all_to_all | solution.py:91
  22.7 17.4 %all-to-all-start.2 = ((bf16[4,16,32,256]{3,2,1,0:T(8,128)(2,1)}), bf16[4,16,32,256]{3,2,1,0:T(8,128)(2,1)S(1)}, u32[]{:S(2)}, u32[]{:S(2)}) async-start(bf16[4,16,32,256]{3,2,1,0:T(8,128)(2,1)} %bitcast.7), calls=%async_computation.2 | async-start | bytes 2097152 | tf_op jit(solution)/shard_map/all_to_all | solution.py:77
  118.5 61.6 %all-to-all-start.3 = ((bf16[16,2,65536]{2,1,0:T(2,128)(2,1)}), bf16[16,2,65536]{2,1,0:T(2,128)(2,1)}, u32[]{:S(2)}, u32[]{:S(2)}) async-start(bf16[16,2,65536]{2,1,0:T(2,128)(2,1)} %reshape.226), calls=%async_computation.3 | async-start | bytes 8388608 | tf_op jit(solution)/shard_map/all_to_all | solution.py:105
  366.7 6.2 %copy-start.2 = (f32[1,2,1024,2,512]{4,2,1,0,3:T(8,128)S(1)}, f32[1,2,1024,2,512]{4,2,1,0,3:T(8,128)}, u32[]{:S(2)}) copy-start(f32[1,2,1024,2,512]{4,2,1,0,3:T(8,128)} %copy.44) | copy-start | bytes 25165828
  372.9 2.8 copy-start.1
where the time goes:
time: 379 us; the launch traced here: 376 us
  local copies, waits for them, and re-layouts  114 us (30%)
  blocking collectives  95.7 us (25%)
  matrix products  47.1 us (12%)
  waiting for transfers between devices  45 us (12%)
  other arithmetic  43.8 us (12%)
  starting transfers between devices  24.2 us (6%)
  loops' own time  5.35 us (1%)
    all_to_all x1, blocking collectives, on_device(): lax.all_to_all(spectra, 'parity', split_axis=3, concat_axis=0, tiled=True)  95.7 us
    all_to_all x1, waiting for transfers between devices, on_device(): lax.all_to_all(owned_grid, 'channel', split_axis=2, concat_axis=1, tiled=...  33.2 us
    unnamed x8, local copies, waits for them, and re-layouts  27.8 us
    another operation x2, local copies, waits for them, and re-layouts, on_device(): owned_grid = owned_grid.reshape(2, chan_dev, tile_dev * pixels)  25.2 us
    dot_general x1, matrix products, on_device(): jnp.einsum('ij,rjc->ric', dft_table, weighted, preferred_element_type=jnp...  22.7 us
    dot_general x8, matrix products, grid_block(): jnp.einsum('nm,rmp->rnp', onehot, values, preferred_element_type=jnp.floa...  22.3 us
    all_to_all x1, local copies, waits for them, and re-layouts, on_device(): lax.all_to_all(owned_grid, 'channel', split_axis=2, concat_axis=1, tiled=...  20.1 us
    another operation x1, other arithmetic  17.7 us
  transfers between devices with their start and end apart: 4, of which 2 were waited for; matrix products, arithmetic and copies ran while one was open for 7% of the time, Pallas kernels for 0%

commit v1 on v0

v1 whole, which is shorter than its diff:
```python
import functools
import math

import jax
import jax.numpy as jnp
from jax import lax
from jax.experimental import pallas as pl
from jax.experimental.pallas import tpu as pltpu
from jax.sharding import PartitionSpec as P

AXES = ("uv", "channel", "parity")
LANES = 128
META = 8


def send_kernel(tile_ref, chan_ref, owner_ref, place_ref, owners_ref, vis_ref, ker_ref, out_ref):
    blocks, doubled, _ = vis_ref.shape
    slots = out_ref.shape[0]

    def clear(index, carry):
        out_ref[index] = jnp.zeros(out_ref.shape[1:], out_ref.dtype)
        return carry

    lax.fori_loop(0, slots, clear, 0, unroll=8)

    place = place_ref[0]
    owner_index = place // 16
    group_local = lax.rem(place, 4)
    lane_slot = owner_index * 4 + group_local
    owners = owners_ref[...]
    tile_iota = (
        lax.broadcasted_iota(jnp.int32, owners.shape, 0) * LANES
        + lax.broadcasted_iota(jnp.int32, owners.shape, 1)
    )
    row_iota = lax.broadcasted_iota(jnp.int32, (META, LANES), 0)
    lane_iota = lax.broadcasted_iota(jnp.int32, (META, LANES), 1)
    lane_here = lane_iota // 16 == lax.rem(lane_slot, 8)
    lane_value = lax.rem(lane_iota, 16) + 1
    for block in range(blocks):
        tile = tile_ref[block]
        owner = owner_ref[tile]
        ahead = jnp.where((owners == owner) & (tile_iota < tile), 1.0, 0.0)
        rank = jnp.sum(ahead).astype(jnp.int32)
        dest = owner * (slots // 4) + rank // 2
        half = lax.rem(rank, 2)
        term = jnp.dot(
            vis_ref[block], ker_ref[block], preferred_element_type=jnp.float32
        ).astype(out_ref.dtype)
        out_ref[dest, :doubled, :] = term[:, :LANES]
        out_ref[dest, doubled : 2 * doubled, :] = term[:, LANES:]
        target = group_local * 64 + chan_ref[block] + lane_value
        meta = jnp.where(lane_here & (row_iota == half * 2 + lane_slot // 8), target, 0)
        out_ref[dest, 2 * doubled :, :] = meta.astype(jnp.float32).astype(out_ref.dtype)


def grid_kernel(got_ref, mix_ref, cross_ref, diff_ref, grid_ref, spec_ref, tail_ref):
    channels = mix_ref.shape[1]
    half = channels // 2
    spread = lax.broadcasted_iota(jnp.int32, (256, 256), 0).astype(jnp.float32) + 1.0

    def gather(chunk, carry):
        for parity in range(2):
            ids = [(u * 16 + chunk * 4 + g) * 2 + parity for u in range(4) for g in range(4)]
            meta = sum(got_ref[i, 64:, :].astype(jnp.float32) for i in ids)
            terms = jnp.concatenate(
                [
                    jnp.concatenate([got_ref[i, 16 * part : 16 * part + 16, :] for i in ids], axis=0)
                    for part in range(4)
                ],
                axis=1,
            )
            for tile in range(2):
                target = jnp.concatenate(
                    [meta[2 * tile : 2 * tile + 1], meta[2 * tile + 1 : 2 * tile + 2]], axis=1
                )
                onehot = (spread == target).astype(jnp.float32).astype(jnp.bfloat16)
                placed = jnp.dot(onehot, terms, preferred_element_type=jnp.float32).astype(
                    jnp.bfloat16
                )
                rows = pl.ds(pl.multiple_of(chunk * 256, 256), 256)
                for part in range(2):
                    grid_ref[2 * tile + part, rows, parity * 256 : parity * 256 + 256] = placed[
                        :, part * 256 : part * 256 + 256
                    ]
        return carry

    lax.fori_loop(0, channels // 256, gather, 0)

    sub = lax.broadcasted_iota(jnp.int32, (8, LANES), 0)
    flip = lax.rem(8 - sub, 8)

    for part in range(4):
        lanes = slice(part * LANES, part * LANES + LANES)
        spec_ref[...] = jnp.dot(
            mix_ref[...], grid_ref[part], preferred_element_type=jnp.float32
        )

        def powers(a_r, a_i, b_r, b_i):
            d_r = a_r - b_r
            d_i = a_i - b_i
            return a_r * b_r + a_i * b_i, d_r * d_r + d_i * d_i

        def pick(row):
            block = spec_ref[pl.ds(row, 8), :]
            return [block[:, k * LANES : (k + 1) * LANES] for k in range(4)]

        mid = pick(half)
        mid_cross, mid_diff = powers(*mid)
        tail_ref[0, half : half + 8, :] = mid_cross
        tail_ref[1, half : half + 8, :] = mid_diff

        def combine(index, carry):
            row = pl.multiple_of(index * 8, 8)
            cos = pick(row)
            sin = pick(pl.multiple_of(half + index * 8, 8))
            keep = (sub > 0) | (index > 0)
            sin = [jnp.where(keep, value, 0.0) for value in sin]
            cross, diff = powers(cos[0] + sin[1], cos[1] - sin[0], cos[2] + sin[3], cos[3] - sin[2])
            cross_ref[pl.ds(row, 8), lanes] = cross
            diff_ref[pl.ds(row, 8), lanes] = diff
            cross, diff = powers(cos[0] - sin[1], cos[1] + sin[0], cos[2] - sin[3], cos[3] + sin[2])
            tail_ref[0, pl.ds(row, 8), :] = cross
            tail_ref[1, pl.ds(row, 8), :] = diff
            return carry

        lax.fori_loop(0, half // 8, combine, 0, unroll=4)

        def reverse(index, carry):
            row = pl.multiple_of(half - index * 8, 8)
            below = pl.multiple_of(half - 8 - index * 8, 8)
            dest = pl.multiple_of(half + index * 8, 8)
            for which, out_ref in ((0, cross_ref), (1, diff_ref)):
                first = jnp.take_along_axis(tail_ref[which, pl.ds(row, 8), :], flip, axis=0)
                rest = jnp.take_along_axis(tail_ref[which, pl.ds(below, 8), :], flip, axis=0)
                out_ref[pl.ds(dest, 8), lanes] = jnp.where(sub == 0, first, rest)
            return carry

        lax.fori_loop(0, half // 8, reverse, 0, unroll=4)


def mixing(inv_cov):
    channels = inv_cov.shape[0]
    half = channels // 2
    rows = jnp.arange(half, dtype=jnp.int32)[:, None]
    cols = jnp.arange(channels, dtype=jnp.int32)[None, :]
    angles = (rows * cols % channels).astype(jnp.float32) * (2.0 * math.pi / channels)
    middle = (1 - 2 * (cols % 2)).astype(jnp.float32)
    table = jnp.concatenate(
        [jnp.cos(angles), jnp.where(rows == 0, middle, jnp.sin(angles))], axis=0
    ).astype(jnp.bfloat16)
    table = table * jnp.bfloat16(1.0 / math.sqrt(channels))
    return jnp.einsum("dc,ck->dk", table, inv_cov, preferred_element_type=jnp.float32).astype(
        jnp.bfloat16
    )


def on_device(visibility, kernel, block_tile, block_chan, tile_owner, inv_cov):
    samples = visibility[0, 0]
    weights = kernel[0, 0]
    blocks, doubled, _ = samples.shape
    devices = lax.axis_size("uv") * lax.axis_size("channel") * lax.axis_size("parity")
    channels = inv_cov.shape[0]
    cells = 512
    place = lax.axis_index(("uv", "channel")).reshape(1).astype(jnp.int32)
    smem = pl.BlockSpec(memory_space=pltpu.SMEM)
    vmem = pl.BlockSpec(memory_space=pltpu.VMEM)
    outgoing = pl.pallas_call(
        send_kernel,
        out_shape=jax.ShapeDtypeStruct((devices, 2 * doubled + META, LANES), jnp.bfloat16),
        in_specs=[smem] * 4 + [vmem] * 3,
        out_specs=vmem,
    )(
        block_tile[0, 0],
        block_chan[0, 0],
        tile_owner,
        place,
        tile_owner.reshape(-1, LANES),
        samples,
        weights,
    )
    received = lax.all_to_all(outgoing, AXES, split_axis=0, concat_axis=0, tiled=True)
    mix = mixing(inv_cov)
    shape = jax.ShapeDtypeStruct((channels, cells), jnp.float32)
    return pl.pallas_call(
        grid_kernel,
        out_shape=(shape, shape),
        in_specs=[vmem] * 2,
        out_specs=(vmem, vmem),
        scratch_shapes=[
            pltpu.VMEM((4, channels, 4 * LANES), jnp.bfloat16),
            pltpu.VMEM((channels, 4 * LANES), jnp.float32),
            pltpu.VMEM((2, channels // 2 + 8, LANES), jnp.float32),
        ],
    )(received, mix)


def solution(mesh):
    placed = (
        P("parity", "channel", "uv", None, None),
        P("parity", "channel", "uv", None, None),
        P("parity", "channel", "uv"),
        P("parity", "channel", "uv"),
        P(),
        P(),
    )
    out = P(None, AXES)
    return jax.shard_map(
        on_device, mesh=mesh, in_specs=placed, out_specs=(out, out), check_vma=False
    )
```

time: 379 us -> 63.2 us (0.17)
  local copies, waits for them, and re-layouts: 114 us -> 0.01 us
  blocking collectives: 95.7 us -> 0 us
  matrix products: 47.1 us -> 3.73 us
  waiting for transfers between devices: 45 us -> 13.2 us
  other arithmetic: 43.8 us -> 15.8 us
  Pallas kernels: 0 us -> 17.6 us
  starting transfers between devices: 24.2 us -> 11.9 us
  loops' own time: 5.35 us -> 0 us
    all_to_all x1 -> x0, blocking collectives: 95.7 us -> none  [on_device(): lax.all_to_all(spectra, 'parity', split_axis=3, concat_axis=0, tiled=True)]
    dot_general x10 -> x1, matrix products: 47.1 us -> 3.73 us  [mixing(): jnp.einsum('dc,ck->dk', table, inv_cov, preferred_element_type=jnp.float32)]
    all_to_all x5 -> x0, local copies, waits for them, and re-layouts: 35.1 us -> none  [the longest x1 20.1 us: on_device(): lax.all_to_all(owned_grid, 'channel', split_axis=2, concat_axis=1, tiled=...]
    all_to_all x4 -> x1, waiting for transfers between devices: 45 us -> 13.2 us  [on_device(): lax.all_to_all(outgoing, AXES, split_axis=0, concat_axis=0, tiled=True)]
    unnamed x8 -> x2, local copies, waits for them, and re-layouts: 27.8 us -> 0.01 us
    another operation x2 -> x0, local copies, waits for them, and re-layouts: 25.2 us -> none  [on_device(): owned_grid = owned_grid.reshape(2, chan_dev, tile_dev * pixels)]
    pallas_call x0 -> x2, Pallas kernels: none -> 17.6 us  [the longest x1 13.6 us: on_device(): pl.pallas_call(grid_kernel, out_shape=(shape, shape), in_specs=[vmem] * 2...]
    all_to_all x4 -> x1, starting transfers between devices: 24.2 us -> 11.9 us  [on_device(): lax.all_to_all(outgoing, AXES, split_axis=0, concat_axis=0, tiled=True)]
  transfers between devices with their start and end apart: 4 -> 1, of which waited for: 2 -> 1; matrix products, arithmetic and copies ran while one was open for 7% -> 31% of each run, Pallas kernels for 0% -> 0%
where the time goes in v1:
time: 63.2 us; the launch traced here: 63 us
  Pallas kernels  17.6 us (28%)
  other arithmetic  15.8 us (25%)
  waiting for transfers between devices  13.2 us (21%)
  starting transfers between devices  11.9 us (19%)
  matrix products  3.73 us (6%)
  between operations  0.69 us (1%)
    another operation x2, other arithmetic  15.8 us
    pallas_call x1, Pallas kernels, on_device(): pl.pallas_call(grid_kernel, out_shape=(shape, shape), in_specs=[vmem] * 2...  13.6 us
    all_to_all x1, waiting for transfers between devices, on_device(): lax.all_to_all(outgoing, AXES, split_axis=0, concat_axis=0, tiled=True)  13.2 us
    all_to_all x1, starting transfers between devices, on_device(): lax.all_to_all(outgoing, AXES, split_axis=0, concat_axis=0, tiled=True)  11.9 us
    pallas_call x1, Pallas kernels, on_device(): pl.pallas_call(send_kernel, out_shape=jax.ShapeDtypeStruct((devices, 2 *...  4.03 us
    dot_general x1, matrix products, mixing(): jnp.einsum('dc,ck->dk', table, inv_cov, preferred_element_type=jnp.float32)  3.73 us
  transfers between devices with their start and end apart: 1, of which 1 were waited for; matrix products, arithmetic and copies ran while one was open for 31% of the time, Pallas kernels for 0%

profile of v1, /device:TPU:1, one launch (start us, length us, event | category | flops | bytes accessed | tf_op | source)
XLA Modules:
  0.0 63.0 jit_solution(8038694048292085484)
XLA Ops:
  0.6 0.0 copy-start
  0.7 4.0 %shard_map.77 = bf16[128,72,128]{2,1,0:T(8,128)(2,1)} custom-call(s32[32]{0:T(128)} %bitcast.10, s32[32]{0:T(128)} %bitcast.11, s32[256]{0:T(256)} %owner_ref.1, s32[1]{0:T(128)} %bitcast.2.place_ref, s32[2,128]{1,0:T(2,128)} %bitcast.9, bf16[32,32,128]{2,1,0:T(8,128)(2,1)} %bitcast.8, bf16[32,128,256]{2,1,0:T(8,128)(2,1)} %bitcast.7), custom_call_target="tpu_custom_call" | custom-call | tf_op jit(solution)/shard_map/pallas_call | solution.py:167
  4.7 11.9 %all-to-all-start = ((bf16[128,72,128]{2,1,0:T(8,128)(2,1)}), bf16[128,72,128]{2,1,0:T(8,128)(2,1)}, u32[]{:S(2)}, u32[]{:S(2)}) async-start(bf16[128,72,128]{2,1,0:T(8,128)(2,1)} %shard_map.77), calls=%async_computation | async-start | bytes 4718592 | tf_op jit(solution)/shard_map/all_to_all | solution.py:181
  16.6 7.8 %cosine_convert_fusion = bf16[512,1024]{1,0:T(8,128)(2,1)S(1)} fusion(), kind=kLoop, calls=%fused_computation.11 | loop fusion | flops 7864320 | bytes 1048576 | tf_op jit(solution)/shard_map/convert
  24.4 8.1 %select_convert_fusion = bf16[512,1024]{1,0:T(8,128)(2,1)S(1)} fusion(bf16[1024]{0:T(1024)(128)(2,1)S(1)} %fusion.13, pred[512]{0:T(512)(128)(4,1)S(1)} %iota_compare_fusion), kind=kLoop, calls=%fused_computation.10 | loop fusion | flops 7864320 | bytes 1051136 | tf_op jit(solution)/shard_map/convert.1
  32.4 0.0 copy-done
  32.5 3.7 %fusion.9.mix_ref = bf16[1024,1024]{1,0:T(8,128)(2,1)} fusion(bf16[1024,1024]{1,0:T(8,128)(2,1)S(1)} %copy-done, bf16[512,1024]{1,0:T(8,128)(2,1)S(1)} %select_convert_fusion, bf16[512,1024]{1,0:T(8,128)(2,1)S(1)} %cosine_convert_fusion), kind=kOutput, calls=%fused_computation.15 | convolution fusion | flops 2154823680 | bytes 6291456 | tf_op jit(solution)/shard_map/dc,ck->dk/dot_general | solution.py:152
  36.2 13.2 %all-to-all-done.got_ref = bf16[128,72,128]{2,1,0:T(8,128)(2,1)} async-done(((bf16[128,72,128]{2,1,0:T(8,128)(2,1)}), bf16[128,72,128]{2,1,0:T(8,128)(2,1)}, u32[]{:S(2)}, u32[]{:S(2)}) %all-to-all-start) | async-done | bytes 2359328 | tf_op jit(solution)/shard_map/all_to_all | solution.py:181
  49.4 13.6 %shard_map.78 = (f32[1024,512]{1,0:T(8,128)}, f32[1024,512]{1,0:T(8,128)}) custom-call(bf16[128,72,128]{2,1,0:T(8,128)(2,1)} %all-to-all-done.got_ref, bf16[1024,1024]{1,0:T(8,128)(2,1)} %fusion.9.mix_ref), custom_call_target="tpu_custom_call" | custom-call | tf_op jit(solution)/shard_map/pallas_call | solution.py:184
  (2 shorter events, 0.0 us)
Async XLA Ops:
  0.6 31.8 %copy-start = (bf16[1024,1024]{1,0:T(8,128)(2,1)S(1)}, bf16[1024,1024]{1,0:T(8,128)(2,1)}, u32[]{:S(2)}) copy-start(bf16[1024,1024]{1,0:T(8,128)(2,1)} %param.11) | copy-start | bytes 6291460
  4.7 44.7 %all-to-all-start = ((bf16[128,72,128]{2,1,0:T(8,128)(2,1)}), bf16[128,72,128]{2,1,0:T(8,128)(2,1)}, u32[]{:S(2)}, u32[]{:S(2)}) async-start(bf16[128,72,128]{2,1,0:T(8,128)(2,1)} %shard_map.77), calls=%async_computation | async-start | bytes 4718592 | tf_op jit(solution)/shard_map/all_to_all | solution.py:181

commit v2 on v1

--- a/solution.py
+++ b/solution.py
@@ -53,12 +53,28 @@
         out_ref[dest, 2 * doubled :, :] = meta.astype(jnp.float32).astype(out_ref.dtype)
 
 
-def grid_kernel(got_ref, mix_ref, cross_ref, diff_ref, grid_ref, spec_ref, tail_ref):
+def grid_kernel(
+    got_hbm, mix_hbm, cross_hbm, diff_hbm, got_ref, mix_ref, grid_ref, even_ref, odd_ref, out_ref,
+    got_sem, mix_sem, out_sem,
+):
     channels = mix_ref.shape[1]
     half = channels // 2
+
+    def fetch(chunk, u):
+        rows = pl.ds((u * 16 + chunk * 4) * 2, 8)
+        return pltpu.make_async_copy(got_hbm.at[rows], got_ref.at[rows], got_sem.at[chunk, u])
+
+    for chunk in range(4):
+        for u in range(4):
+            fetch(chunk, u).start()
+    mix_copy = pltpu.make_async_copy(mix_hbm, mix_ref, mix_sem)
+    mix_copy.start()
+
     spread = lax.broadcasted_iota(jnp.int32, (256, 256), 0).astype(jnp.float32) + 1.0
 
     def gather(chunk, carry):
+        for u in range(4):
+            fetch(chunk, u).wait()
         for parity in range(2):
             ids = [(u * 16 + chunk * 4 + g) * 2 + parity for u in range(4) for g in range(4)]
             meta = sum(got_ref[i, 64:, :].astype(jnp.float32) for i in ids)
@@ -69,73 +85,79 @@
                 ],
                 axis=1,
             )
+            onehot = []
             for tile in range(2):
                 target = jnp.concatenate(
                     [meta[2 * tile : 2 * tile + 1], meta[2 * tile + 1 : 2 * tile + 2]], axis=1
                 )
-                onehot = (spread == target).astype(jnp.float32).astype(jnp.bfloat16)
-                placed = jnp.dot(onehot, terms, preferred_element_type=jnp.float32).astype(
-                    jnp.bfloat16
-                )
-                rows = pl.ds(pl.multiple_of(chunk * 256, 256), 256)
+                onehot.append((spread == target).astype(jnp.float32).astype(jnp.bfloat16))
+            placed = jnp.dot(
+                jnp.concatenate(onehot, axis=0), terms, preferred_element_type=jnp.float32
+            ).astype(jnp.bfloat16)
+            rows = pl.ds(pl.multiple_of(chunk * 256, 256), 256)
+            for tile in range(2):
                 for part in range(2):
                     grid_ref[2 * tile + part, rows, parity * 256 : parity * 256 + 256] = placed[
-                        :, part * 256 : part * 256 + 256
+                        tile * 256 : tile * 256 + 256, part * 256 : part * 256 + 256
                     ]
         return carry
 
     lax.fori_loop(0, channels // 256, gather, 0)
+    mix_copy.wait()
 
     sub = lax.broadcasted_iota(jnp.int32, (8, LANES), 0)
     flip = lax.rem(8 - sub, 8)
 
-    for part in range(4):
-        lanes = slice(part * LANES, part * LANES + LANES)
+    def powers(a_r, a_i, b_r, b_i):
+        d_r = a_r - b_r
+        d_i = a_i - b_i
+        return a_r * b_r + a_i * b_i, d_r * d_r + d_i * d_i
+
+    def combine(part, spec_ref):
+        for index in range(half // 8):
+            row = index * 8
+            cos = [spec_ref[row : row + 8, k * LANES : (k + 1) * LANES] for k in range(4)]
+            sin = [
+                spec_ref[half + row : half + row + 8, k * LANES : (k + 1) * LANES] for k in range(4)
+            ]
+            if index == 0:
+                for which, power in enumerate(powers(*sin)):
+                    out_ref[part, which, half : half + 1, :] = power[:1]
+                sin = [jnp.where(sub > 0, value, 0.0) for value in sin]
+            lower = powers(cos[0] + sin[1], cos[1] - sin[0], cos[2] + sin[3], cos[3] - sin[2])
+            upper = powers(cos[0] - sin[1], cos[1] + sin[0], cos[2] - sin[3], cos[3] + sin[2])
+            top = channels - row
+            for which in range(2):
+                out_ref[part, which, row : row + 8, :] = lower[which]
+                mirrored = jnp.take_along_axis(upper[which], flip, axis=0)
+                out_ref[part, which, top - 7 : top, :] = mirrored[1:]
+                if index > 0:
+                    out_ref[part, which, top : top + 1, :] = mirrored[:1]
+
+    def product(part, spec_ref):
         spec_ref[...] = jnp.dot(
             mix_ref[...], grid_ref[part], preferred_element_type=jnp.float32
         )
 
-        def powers(a_r, a_i, b_r, b_i):
-            d_r = a_r - b_r
-            d_i = a_i - b_i
-            return a_r * b_r + a_i * b_i, d_r * d_r + d_i * d_i
-
-        def pick(row):
-            block = spec_ref[pl.ds(row, 8), :]
-            return [block[:, k * LANES : (k + 1) * LANES] for k in range(4)]
-
-        mid = pick(half)
-        mid_cross, mid_diff = powers(*mid)
-        tail_ref[0, half : half + 8, :] = mid_cross
-        tail_ref[1, half : half + 8, :] = mid_diff
-
-        def combine(index, carry):
-            row = pl.multiple_of(index * 8, 8)
-            cos = pick(row)
-            sin = pick(pl.multiple_of(half + index * 8, 8))
-            keep = (sub > 0) | (index > 0)
-            sin = [jnp.where(keep, value, 0.0) for value in sin]
-            cross, diff = powers(cos[0] + sin[1], cos[1] - sin[0], cos[2] + sin[3], cos[3] - sin[2])
-            cross_ref[pl.ds(row, 8), lanes] = cross
-            diff_ref[pl.ds(row, 8), lanes] = diff
-            cross, diff = powers(cos[0] - sin[1], cos[1] + sin[0], cos[2] - sin[3], cos[3] + sin[2])
-            tail_ref[0, pl.ds(row, 8), :] = cross
-            tail_ref[1, pl.ds(row, 8), :] = diff
-            return carry
-
-        lax.fori_loop(0, half // 8, combine, 0, unroll=4)
-
-        def reverse(index, carry):
-            row = pl.multiple_of(half - index * 8, 8)
-            below = pl.multiple_of(half - 8 - index * 8, 8)
-            dest = pl.multiple_of(half + index * 8, 8)
-            for which, out_ref in ((0, cross_ref), (1, diff_ref)):
-                first = jnp.take_along_axis(tail_ref[which, pl.ds(row, 8), :], flip, axis=0)
-                rest = jnp.take_along_axis(tail_ref[which, pl.ds(below, 8), :], flip, axis=0)
-                out_ref[pl.ds(dest, 8), lanes] = jnp.where(sub == 0, first, rest)
-            return carry
-
-        lax.fori_loop(0, half // 8, reverse, 0, unroll=4)
+    def send(part, which):
+        target = (cross_hbm, diff_hbm)[which]
+        return pltpu.make_async_copy(
+            out_ref.at[part, which],
+            target.at[:, pl.ds(part * LANES, LANES)],
+            out_sem.at[part, which],
+        )
+
+    specs = (even_ref, odd_ref)
+    product(0, specs[0])
+    for part in range(4):
+        if part < 3:
+            product(part + 1, specs[(part + 1) % 2])
+        combine(part, specs[part % 2])
+        for which in range(2):
+            send(part, which).start()
+    for part in range(4):
+        for which in range(2):
+            send(part, which).wait()
 
 
 def mixing(inv_cov):
@@ -181,15 +203,22 @@
     received = lax.all_to_all(outgoing, AXES, split_axis=0, concat_axis=0, tiled=True)
     mix = mixing(inv_cov)
     shape = jax.ShapeDtypeStruct((channels, cells), jnp.float32)
+    hbm = pl.BlockSpec(memory_space=pl.ANY)
     return pl.pallas_call(
         grid_kernel,
         out_shape=(shape, shape),
-        in_specs=[vmem] * 2,
-        out_specs=(vmem, vmem),
+        in_specs=[hbm] * 2,
+        out_specs=(hbm, hbm),
         scratch_shapes=[
+            pltpu.VMEM(received.shape, jnp.bfloat16),
+            pltpu.VMEM(mix.shape, jnp.bfloat16),
             pltpu.VMEM((4, channels, 4 * LANES), jnp.bfloat16),
             pltpu.VMEM((channels, 4 * LANES), jnp.float32),
-            pltpu.VMEM((2, channels // 2 + 8, LANES), jnp.float32),
+            pltpu.VMEM((channels, 4 * LANES), jnp.float32),
+            pltpu.VMEM((4, 2, channels, LANES), jnp.float32),
+            pltpu.SemaphoreType.DMA((4, 4)),
+            pltpu.SemaphoreType.DMA,
+            pltpu.SemaphoreType.DMA((4, 2)),
         ],
     )(received, mix)
 

time: 63.2 us -> 58.8 us (0.930)
  Pallas kernels: 17.6 us -> 13.2 us
    pallas_call x1, Pallas kernels: 13.6 us -> 9.18 us  [on_device(): pl.pallas_call(grid_kernel, out_shape=(shape, shape), in_specs=[hbm] * 2,...]
  transfers between devices with their start and end apart: 1 -> 1, of which waited for: 1 -> 1; matrix products, arithmetic and copies ran while one was open for 31% -> 33% of each run, Pallas kernels for 0% -> 0%
where the time goes in v2:
time: 58.8 us; the launch traced here: 58.6 us
  other arithmetic  15.8 us (27%)
  Pallas kernels  13.2 us (22%)
  waiting for transfers between devices  13.2 us (22%)
  starting transfers between devices  11.9 us (20%)
  matrix products  3.73 us (6%)
  between operations  0.69 us (1%)
    another operation x2, other arithmetic  15.8 us
    all_to_all x1, waiting for transfers between devices, on_device(): lax.all_to_all(outgoing, AXES, split_axis=0, concat_axis=0, tiled=True)  13.2 us
    all_to_all x1, starting transfers between devices, on_device(): lax.all_to_all(outgoing, AXES, split_axis=0, concat_axis=0, tiled=True)  11.9 us
    pallas_call x1, Pallas kernels, on_device(): pl.pallas_call(grid_kernel, out_shape=(shape, shape), in_specs=[hbm] * 2,...  9.18 us
    pallas_call x1, Pallas kernels, on_device(): pl.pallas_call(send_kernel, out_shape=jax.ShapeDtypeStruct((devices, 2 *...  4.03 us
    dot_general x1, matrix products, mixing(): jnp.einsum('dc,ck->dk', table, inv_cov, preferred_element_type=jnp.float32)  3.73 us
  transfers between devices with their start and end apart: 1, of which 1 were waited for; matrix products, arithmetic and copies ran while one was open for 33% of the time, Pallas kernels for 0%

profile of v2, /device:TPU:1, one launch (start us, length us, event | category | flops | bytes accessed | tf_op | source)
XLA Modules:
  0.0 58.6 jit_solution(11800589721267895721)
XLA Ops:
  0.6 0.0 copy-start
  0.7 4.0 %shard_map.77 = bf16[128,72,128]{2,1,0:T(8,128)(2,1)} custom-call(s32[32]{0:T(128)} %bitcast.10, s32[32]{0:T(128)} %bitcast.11, s32[256]{0:T(256)} %owner_ref.1, s32[1]{0:T(128)} %bitcast.2.place_ref, s32[2,128]{1,0:T(2,128)} %bitcast.9, bf16[32,32,128]{2,1,0:T(8,128)(2,1)} %bitcast.8, bf16[32,128,256]{2,1,0:T(8,128)(2,1)} %bitcast.7), custom_call_target="tpu_custom_call" | custom-call | tf_op jit(solution)/shard_map/pallas_call | solution.py:189
  4.7 11.9 %all-to-all-start = ((bf16[128,72,128]{2,1,0:T(8,128)(2,1)}), bf16[128,72,128]{2,1,0:T(8,128)(2,1)}, u32[]{:S(2)}, u32[]{:S(2)}) async-start(bf16[128,72,128]{2,1,0:T(8,128)(2,1)} %shard_map.77), calls=%async_computation | async-start | bytes 4718592 | tf_op jit(solution)/shard_map/all_to_all | solution.py:203
  16.6 7.8 %cosine_convert_fusion = bf16[512,1024]{1,0:T(8,128)(2,1)S(1)} fusion(), kind=kLoop, calls=%fused_computation.11 | loop fusion | flops 7864320 | bytes 1048576 | tf_op jit(solution)/shard_map/convert
  24.4 8.1 %select_convert_fusion = bf16[512,1024]{1,0:T(8,128)(2,1)S(1)} fusion(bf16[1024]{0:T(1024)(128)(2,1)S(1)} %fusion.13, pred[512]{0:T(512)(128)(4,1)S(1)} %iota_compare_fusion), kind=kLoop, calls=%fused_computation.10 | loop fusion | flops 7864320 | bytes 1051136 | tf_op jit(solution)/shard_map/convert.1
  32.4 0.0 copy-done
  32.5 3.7 %fusion.9.mix_hbm = bf16[1024,1024]{1,0:T(8,128)(2,1)} fusion(bf16[1024,1024]{1,0:T(8,128)(2,1)S(1)} %copy-done, bf16[512,1024]{1,0:T(8,128)(2,1)S(1)} %select_convert_fusion, bf16[512,1024]{1,0:T(8,128)(2,1)S(1)} %cosine_convert_fusion), kind=kOutput, calls=%fused_computation.15 | convolution fusion | flops 2154823680 | bytes 6291456 | tf_op jit(solution)/shard_map/dc,ck->dk/dot_general | solution.py:174
  36.2 13.2 %all-to-all-done.got_hbm = bf16[128,72,128]{2,1,0:T(8,128)(2,1)} async-done(((bf16[128,72,128]{2,1,0:T(8,128)(2,1)}), bf16[128,72,128]{2,1,0:T(8,128)(2,1)}, u32[]{:S(2)}, u32[]{:S(2)}) %all-to-all-start) | async-done | bytes 2359328 | tf_op jit(solution)/shard_map/all_to_all | solution.py:203
  49.4 9.2 %shard_map.78 = (f32[1024,512]{1,0:T(8,128)}, f32[1024,512]{1,0:T(8,128)}) custom-call(bf16[128,72,128]{2,1,0:T(8,128)(2,1)} %all-to-all-done.got_hbm, bf16[1024,1024]{1,0:T(8,128)(2,1)} %fusion.9.mix_hbm), custom_call_target="tpu_custom_call" | custom-call | tf_op jit(solution)/shard_map/pallas_call | solution.py:207
  (2 shorter events, 0.0 us)
Async XLA Ops:
  0.6 31.8 %copy-start = (bf16[1024,1024]{1,0:T(8,128)(2,1)S(1)}, bf16[1024,1024]{1,0:T(8,128)(2,1)}, u32[]{:S(2)}) copy-start(bf16[1024,1024]{1,0:T(8,128)(2,1)} %param.11) | copy-start | bytes 6291460
  4.7 44.7 %all-to-all-start = ((bf16[128,72,128]{2,1,0:T(8,128)(2,1)}), bf16[128,72,128]{2,1,0:T(8,128)(2,1)}, u32[]{:S(2)}, u32[]{:S(2)}) async-start(bf16[128,72,128]{2,1,0:T(8,128)(2,1)} %shard_map.77), calls=%async_computation | async-start | bytes 4718592 | tf_op jit(solution)/shard_map/all_to_all | solution.py:203

commit v3 on v2

--- a/solution.py
+++ b/solution.py
@@ -10,6 +10,8 @@
 
 AXES = ("uv", "channel", "parity")
 LANES = 128
+LIMIT = 48
+SPARE = 8
 META = 8
 
 
@@ -54,27 +56,18 @@
 
 
 def grid_kernel(
-    got_hbm, mix_hbm, cross_hbm, diff_hbm, got_ref, mix_ref, grid_ref, even_ref, odd_ref, out_ref,
-    got_sem, mix_sem, out_sem,
+    got_ref, mix_hbm, cross_hbm, diff_hbm, mix_ref, grid_ref, even_ref, odd_ref, out_ref,
+    mix_sem, out_sem,
 ):
     channels = mix_ref.shape[1]
     half = channels // 2
 
-    def fetch(chunk, u):
-        rows = pl.ds((u * 16 + chunk * 4) * 2, 8)
-        return pltpu.make_async_copy(got_hbm.at[rows], got_ref.at[rows], got_sem.at[chunk, u])
-
-    for chunk in range(4):
-        for u in range(4):
-            fetch(chunk, u).start()
-    mix_copy = pltpu.make_async_copy(mix_hbm, mix_ref, mix_sem)
+    mix_copy = pltpu.make_async_copy(mix_hbm.at[0], mix_ref, mix_sem)
     mix_copy.start()
 
     spread = lax.broadcasted_iota(jnp.int32, (256, 256), 0).astype(jnp.float32) + 1.0
 
     def gather(chunk, carry):
-        for u in range(4):
-            fetch(chunk, u).wait()
         for parity in range(2):
             ids = [(u * 16 + chunk * 4 + g) * 2 + parity for u in range(4) for g in range(4)]
             meta = sum(got_ref[i, 64:, :].astype(jnp.float32) for i in ids)
@@ -160,20 +153,40 @@
             send(part, which).wait()
 
 
-def mixing(inv_cov):
-    channels = inv_cov.shape[0]
+def mix_kernel(cov_ref, out_hbm, table_ref, out_ref, sem):
+    channels = cov_ref.shape[0]
     half = channels // 2
-    rows = jnp.arange(half, dtype=jnp.int32)[:, None]
-    cols = jnp.arange(channels, dtype=jnp.int32)[None, :]
-    angles = (rows * cols % channels).astype(jnp.float32) * (2.0 * math.pi / channels)
-    middle = (1 - 2 * (cols % 2)).astype(jnp.float32)
-    table = jnp.concatenate(
-        [jnp.cos(angles), jnp.where(rows == 0, middle, jnp.sin(angles))], axis=0
-    ).astype(jnp.bfloat16)
-    table = table * jnp.bfloat16(1.0 / math.sqrt(channels))
-    return jnp.einsum("dc,ck->dk", table, inv_cov, preferred_element_type=jnp.float32).astype(
-        jnp.bfloat16
-    )
+    inner = 32
+    scale = 1.0 / math.sqrt(channels)
+
+    def angles(count, step):
+        rows = lax.broadcasted_iota(jnp.int32, (count, channels), 0) * step
+        cols = lax.broadcasted_iota(jnp.int32, (count, channels), 1)
+        return lax.rem(rows * cols, channels).astype(jnp.float32) * (2.0 * math.pi / channels)
+
+    outer_angles = angles(half // inner, inner)
+    inner_angles = angles(inner, 1)
+    outer_cos, outer_sin = jnp.cos(outer_angles) * scale, jnp.sin(outer_angles) * scale
+    inner_cos, inner_sin = jnp.cos(inner_angles), jnp.sin(inner_angles)
+    for index in range(half // inner):
+        cos, sin = outer_cos[index : index + 1], outer_sin[index : index + 1]
+        lower = cos * inner_cos - sin * inner_sin
+        upper = sin * inner_cos + cos * inner_sin
+        if index == 0:
+            rows = lax.broadcasted_iota(jnp.int32, upper.shape, 0)
+            odd = lax.rem(lax.broadcasted_iota(jnp.int32, upper.shape, 1), 2)
+            middle = (1 - 2 * odd).astype(jnp.float32) * scale
+            upper = jnp.where(rows == 0, middle, upper)
+        table_ref[index * inner : index * inner + inner, :] = lower.astype(table_ref.dtype)
+        table_ref[half + index * inner : half + index * inner + inner, :] = upper.astype(
+            table_ref.dtype
+        )
+    out_ref[...] = jnp.dot(
+        table_ref[...], cov_ref[...], preferred_element_type=jnp.float32
+    ).astype(out_ref.dtype)
+    copy = pltpu.make_async_copy(out_ref, out_hbm.at[0], sem)
+    copy.start()
+    copy.wait()
 
 
 def on_device(visibility, kernel, block_tile, block_chan, tile_owner, inv_cov):
@@ -186,6 +199,7 @@
     place = lax.axis_index(("uv", "channel")).reshape(1).astype(jnp.int32)
     smem = pl.BlockSpec(memory_space=pltpu.SMEM)
     vmem = pl.BlockSpec(memory_space=pltpu.VMEM)
+    hbm = pl.BlockSpec(memory_space=pl.ANY)
     outgoing = pl.pallas_call(
         send_kernel,
         out_shape=jax.ShapeDtypeStruct((devices, 2 * doubled + META, LANES), jnp.bfloat16),
@@ -201,25 +215,36 @@
         weights,
     )
     received = lax.all_to_all(outgoing, AXES, split_axis=0, concat_axis=0, tiled=True)
-    mix = mixing(inv_cov)
+    mix = pl.pallas_call(
+        mix_kernel,
+        out_shape=jax.ShapeDtypeStruct((SPARE,) + inv_cov.shape, inv_cov.dtype),
+        in_specs=[vmem],
+        out_specs=hbm,
+        scratch_shapes=[
+            pltpu.VMEM(inv_cov.shape, inv_cov.dtype),
+            pltpu.VMEM(inv_cov.shape, inv_cov.dtype),
+            pltpu.SemaphoreType.DMA,
+        ],
+        cost_estimate=pl.CostEstimate(
+            flops=2 * channels**3, bytes_accessed=4 * channels**2, transcendentals=0
+        ),
+    )(inv_cov)
     shape = jax.ShapeDtypeStruct((channels, cells), jnp.float32)
-    hbm = pl.BlockSpec(memory_space=pl.ANY)
     return pl.pallas_call(
         grid_kernel,
         out_shape=(shape, shape),
-        in_specs=[hbm] * 2,
+        in_specs=[vmem, hbm],
         out_specs=(hbm, hbm),
         scratch_shapes=[
-            pltpu.VMEM(received.shape, jnp.bfloat16),
-            pltpu.VMEM(mix.shape, jnp.bfloat16),
+            pltpu.VMEM(inv_cov.shape, jnp.bfloat16),
             pltpu.VMEM((4, channels, 4 * LANES), jnp.bfloat16),
             pltpu.VMEM((channels, 4 * LANES), jnp.float32),
             pltpu.VMEM((channels, 4 * LANES), jnp.float32),
             pltpu.VMEM((4, 2, channels, LANES), jnp.float32),
-            pltpu.SemaphoreType.DMA((4, 4)),
             pltpu.SemaphoreType.DMA,
             pltpu.SemaphoreType.DMA((4, 2)),
         ],
+        compiler_params=pltpu.CompilerParams(vmem_limit_bytes=LIMIT * 2**20),
     )(received, mix)
 
 

time: 58.8 us -> 57.3 us (0.974)
  other arithmetic: 15.8 us -> 0 us
  waiting for transfers between devices: 13.2 us -> 27.2 us
  Pallas kernels: 13.2 us -> 17.7 us
  matrix products: 3.73 us -> 0 us
    another operation x2 -> x0, other arithmetic: 15.8 us -> none
    all_to_all x1, waiting for transfers between devices: 13.2 us -> 27.2 us  [on_device(): lax.all_to_all(outgoing, AXES, split_axis=0, concat_axis=0, tiled=True)]
    pallas_call x1 -> x2, Pallas kernels: 9.18 us -> 13.8 us  [the longest x1 7.88 us: on_device(): pl.pallas_call(grid_kernel, out_shape=(shape, shape), in_specs=[vmem, hbm...]
    dot_general x1 -> x0, matrix products: 3.73 us -> none  [mixing(): jnp.einsum('dc,ck->dk', table, inv_cov, preferred_element_type=jnp.float32)]
  transfers between devices with their start and end apart: 1 -> 1, of which waited for: 1 -> 1; matrix products, arithmetic and copies ran while one was open for 33% -> 0% of each run, Pallas kernels for 0% -> 10%
where the time goes in v3:
time: 57.3 us; the launch traced here: 57 us
  waiting for transfers between devices  27.2 us (47%)
  Pallas kernels  17.7 us (31%)
  starting transfers between devices  11.5 us (20%)
  between operations  0.65 us (1%)
    all_to_all x1, waiting for transfers between devices, on_device(): lax.all_to_all(outgoing, AXES, split_axis=0, concat_axis=0, tiled=True)  27.2 us
    all_to_all x1, starting transfers between devices, on_device(): lax.all_to_all(outgoing, AXES, split_axis=0, concat_axis=0, tiled=True)  11.5 us
    pallas_call x1, Pallas kernels, on_device(): pl.pallas_call(grid_kernel, out_shape=(shape, shape), in_specs=[vmem, hbm...  7.88 us
    pallas_call x1, Pallas kernels, on_device(): pl.pallas_call(mix_kernel, out_shape=jax.ShapeDtypeStruct((SPARE,) + inv_...  5.91 us
    pallas_call x1, Pallas kernels, on_device(): pl.pallas_call(send_kernel, out_shape=jax.ShapeDtypeStruct((devices, 2 *...  3.91 us
  transfers between devices with their start and end apart: 1, of which 1 were waited for; matrix products, arithmetic and copies ran while one was open for 0% of the time, Pallas kernels for 10%

profile of v3, /device:TPU:1, one launch (start us, length us, event | category | flops | bytes accessed | tf_op | source)
XLA Modules:
  0.0 57.0 jit_solution(3225134672267549901)
XLA Ops:
  0.6 3.9 %shard_map.77 = bf16[128,72,128]{2,1,0:T(8,128)(2,1)} custom-call(s32[32]{0:T(128)} %bitcast.9, s32[32]{0:T(128)} %bitcast.10, s32[256]{0:T(256)} %owner_ref.1, s32[1]{0:T(128)} %bitcast.2.place_ref, s32[2,128]{1,0:T(2,128)} %bitcast.8, bf16[32,32,128]{2,1,0:T(8,128)(2,1)} %bitcast.7, bf16[32,128,256]{2,1,0:T(8,128)(2,1)} %bitcast.6), custom_call_target="tpu_custom_call" | custom-call | tf_op jit(solution)/shard_map/pallas_call | solution.py:203
  4.5 11.5 %all-to-all-start = ((bf16[128,72,128]{2,1,0:T(8,128)(2,1)}), bf16[128,72,128]{2,1,0:T(8,128)(2,1)S(1)}, u32[]{:S(2)}, u32[]{:S(2)}) async-start(bf16[128,72,128]{2,1,0:T(8,128)(2,1)} %shard_map.77), calls=%async_computation | async-start | bytes 4718592 | tf_op jit(solution)/shard_map/all_to_all | solution.py:217
  16.0 5.9 %shard_map.78.mix_hbm = bf16[8,1024,1024]{2,1,0:T(8,128)(2,1)} custom-call(bf16[1024,1024]{1,0:T(8,128)(2,1)} %cov_ref.1), custom_call_target="tpu_custom_call" | custom-call | flops 2147483648 | bytes 4194304 | tf_op jit(solution)/shard_map/pallas_call | solution.py:218
  22.0 27.2 %all-to-all-done.got_ref = bf16[128,72,128]{2,1,0:T(8,128)(2,1)S(1)} async-done(((bf16[128,72,128]{2,1,0:T(8,128)(2,1)}), bf16[128,72,128]{2,1,0:T(8,128)(2,1)S(1)}, u32[]{:S(2)}, u32[]{:S(2)}) %all-to-all-start) | async-done | bytes 2359328 | tf_op jit(solution)/shard_map/all_to_all | solution.py:217
  49.2 7.9 %shard_map.79 = (f32[1024,512]{1,0:T(8,128)}, f32[1024,512]{1,0:T(8,128)}) custom-call(bf16[128,72,128]{2,1,0:T(8,128)(2,1)S(1)} %all-to-all-done.got_ref, bf16[8,1024,1024]{2,1,0:T(8,128)(2,1)} %shard_map.78.mix_hbm), custom_call_target="tpu_custom_call" | custom-call | tf_op jit(solution)/shard_map/pallas_call | solution.py:233
Async XLA Ops:
  4.5 44.6 %all-to-all-start = ((bf16[128,72,128]{2,1,0:T(8,128)(2,1)}), bf16[128,72,128]{2,1,0:T(8,128)(2,1)S(1)}, u32[]{:S(2)}, u32[]{:S(2)}) async-start(bf16[128,72,128]{2,1,0:T(8,128)(2,1)} %shard_map.77), calls=%async_computation | async-start | bytes 4718592 | tf_op jit(solution)/shard_map/all_to_all | solution.py:217

commit v4 on v3

--- a/solution.py
+++ b/solution.py
@@ -12,51 +12,79 @@
 LANES = 128
 LIMIT = 48
 SPARE = 8
-META = 8
-
-
-def send_kernel(tile_ref, chan_ref, owner_ref, place_ref, owners_ref, vis_ref, ker_ref, out_ref):
+PAIR = 2
+
+
+def rows_of(ref, slot):
+    return ref.at[slot].reshape(ref.shape[1] * PAIR, LANES)
+
+
+def send_kernel(
+    tile_ref, chan_ref, owner_ref, place_ref, owners_ref, vis_hbm, ker_hbm, out_ref,
+    vis_ref, ker_ref, zero_ref, vis_sem, ker_sem, zero_sem,
+):
     blocks, doubled, _ = vis_ref.shape
     slots = out_ref.shape[0]
-
-    def clear(index, carry):
-        out_ref[index] = jnp.zeros(out_ref.shape[1:], out_ref.dtype)
-        return carry
-
-    lax.fori_loop(0, slots, clear, 0, unroll=8)
+    clear = zero_ref.shape[0]
+    loads = ker_sem.shape[0]
+    size = blocks // loads
+
+    vis_copy = pltpu.make_async_copy(vis_hbm, vis_ref, vis_sem)
+    vis_copy.start()
+    ker_copies = []
+    for load in range(loads):
+        span = pl.ds(load * size, size)
+        ker_copies.append(
+            pltpu.make_async_copy(ker_hbm.at[span], ker_ref.at[span], ker_sem.at[load])
+        )
+        ker_copies[-1].start()
+
+    zero_ref[...] = jnp.zeros(zero_ref.shape, zero_ref.dtype)
+    zero_copies = []
+    for index in range(slots // clear):
+        target = out_ref.at[pl.ds(index * clear, clear)]
+        zero_copies.append(pltpu.make_async_copy(zero_ref, target, zero_sem.at[index]))
+        zero_copies[-1].start()
 
     place = place_ref[0]
-    owner_index = place // 16
     group_local = lax.rem(place, 4)
-    lane_slot = owner_index * 4 + group_local
+    lane_slot = place // 16 * 4 + group_local
     owners = owners_ref[...]
     tile_iota = (
         lax.broadcasted_iota(jnp.int32, owners.shape, 0) * LANES
         + lax.broadcasted_iota(jnp.int32, owners.shape, 1)
     )
-    row_iota = lax.broadcasted_iota(jnp.int32, (META, LANES), 0)
-    lane_iota = lax.broadcasted_iota(jnp.int32, (META, LANES), 1)
-    lane_here = lane_iota // 16 == lax.rem(lane_slot, 8)
-    lane_value = lax.rem(lane_iota, 16) + 1
+    row_iota = lax.broadcasted_iota(jnp.int32, (PAIR, LANES), 0)
+    lane_iota = lax.broadcasted_iota(jnp.int32, (PAIR, LANES), 1)
+    lane_here = (lane_iota // 16 == lax.rem(lane_slot, 8)) & (row_iota == lane_slot // 8)
+    lane_value = lax.rem(lane_iota, 16) + 1 + group_local * 64
+    dests, metas = [], []
     for block in range(blocks):
         tile = tile_ref[block]
         owner = owner_ref[tile]
         ahead = jnp.where((owners == owner) & (tile_iota < tile), 1.0, 0.0)
         rank = jnp.sum(ahead).astype(jnp.int32)
-        dest = owner * (slots // 4) + rank // 2
-        half = lax.rem(rank, 2)
-        term = jnp.dot(
-            vis_ref[block], ker_ref[block], preferred_element_type=jnp.float32
-        ).astype(out_ref.dtype)
-        out_ref[dest, :doubled, :] = term[:, :LANES]
-        out_ref[dest, doubled : 2 * doubled, :] = term[:, LANES:]
-        target = group_local * 64 + chan_ref[block] + lane_value
-        meta = jnp.where(lane_here & (row_iota == half * 2 + lane_slot // 8), target, 0)
-        out_ref[dest, 2 * doubled :, :] = meta.astype(jnp.float32).astype(out_ref.dtype)
+        dests.append(owner * (slots // 4) + rank // 2)
+        target = (chan_ref[block] + lane_value) * (1 - 2 * lax.rem(rank, 2))
+        metas.append(jnp.where(lane_here, target, 0).astype(jnp.float32).astype(out_ref.dtype))
+
+    vis_copy.wait()
+    for copy in zero_copies:
+        copy.wait()
+    for load in range(loads):
+        ker_copies[load].wait()
+        for block in range(load * size, load * size + size):
+            term = jnp.dot(
+                vis_ref[block], ker_ref[block], preferred_element_type=jnp.float32
+            ).astype(out_ref.dtype)
+            slot = rows_of(out_ref, dests[block])
+            slot[:doubled, :] = term[:, :LANES]
+            slot[doubled : 2 * doubled, :] = term[:, LANES:]
+            slot[2 * doubled :, :] = metas[block]
 
 
 def grid_kernel(
-    got_ref, mix_hbm, cross_hbm, diff_hbm, mix_ref, grid_ref, even_ref, odd_ref, out_ref,
+    got_ref, mix_hbm, cross_hbm, diff_hbm, mix_ref, grid_ref, out_ref,
     mix_sem, out_sem,
 ):
     channels = mix_ref.shape[1]
@@ -67,23 +95,32 @@
 
     spread = lax.broadcasted_iota(jnp.int32, (256, 256), 0).astype(jnp.float32) + 1.0
 
+    height = 66
+    step = 8 * height
+
     def gather(chunk, carry):
+        near = got_ref.at[pl.ds(pl.multiple_of(chunk * step, 16), got_ref.shape[0] - 3 * step)]
         for parity in range(2):
-            ids = [(u * 16 + chunk * 4 + g) * 2 + parity for u in range(4) for g in range(4)]
-            meta = sum(got_ref[i, 64:, :].astype(jnp.float32) for i in ids)
+            ids = [(u * 16 + g) * 2 + parity for u in range(4) for g in range(4)]
+            meta = sum(near[i * height + 64 : i * height + 66, :].astype(jnp.float32) for i in ids)
             terms = jnp.concatenate(
                 [
-                    jnp.concatenate([got_ref[i, 16 * part : 16 * part + 16, :] for i in ids], axis=0)
+                    jnp.concatenate(
+                        [
+                            near[i * height + 16 * part : i * height + 16 * part + 16, :]
+                            for i in ids
+                        ],
+                        axis=0,
+                    )
                     for part in range(4)
                 ],
                 axis=1,
             )
-            onehot = []
-            for tile in range(2):
-                target = jnp.concatenate(
-                    [meta[2 * tile : 2 * tile + 1], meta[2 * tile + 1 : 2 * tile + 2]], axis=1
-                )
-                onehot.append((spread == target).astype(jnp.float32).astype(jnp.bfloat16))
+            target = jnp.concatenate([meta[:1], meta[1:]], axis=1)
+            onehot = [
+                (spread == signed).astype(jnp.float32).astype(jnp.bfloat16)
+                for signed in (target, -target)
+            ]
             placed = jnp.dot(
                 jnp.concatenate(onehot, axis=0), terms, preferred_element_type=jnp.float32
             ).astype(jnp.bfloat16)
@@ -106,13 +143,11 @@
         d_i = a_i - b_i
         return a_r * b_r + a_i * b_i, d_r * d_r + d_i * d_i
 
-    def combine(part, spec_ref):
+    def combine(part, spec):
         for index in range(half // 8):
             row = index * 8
-            cos = [spec_ref[row : row + 8, k * LANES : (k + 1) * LANES] for k in range(4)]
-            sin = [
-                spec_ref[half + row : half + row + 8, k * LANES : (k + 1) * LANES] for k in range(4)
-            ]
+            cos = [spec[row : row + 8, k * LANES : (k + 1) * LANES] for k in range(4)]
+            sin = [spec[half + row : half + row + 8, k * LANES : (k + 1) * LANES] for k in range(4)]
             if index == 0:
                 for which, power in enumerate(powers(*sin)):
                     out_ref[part, which, half : half + 1, :] = power[:1]
@@ -122,15 +157,13 @@
             top = channels - row
             for which in range(2):
                 out_ref[part, which, row : row + 8, :] = lower[which]
-                mirrored = jnp.take_along_axis(upper[which], flip, axis=0)
+                mirrored = jnp.take_along_axis(upper[which], flip, axis=0, mode="promise_in_bounds")
                 out_ref[part, which, top - 7 : top, :] = mirrored[1:]
                 if index > 0:
                     out_ref[part, which, top : top + 1, :] = mirrored[:1]
 
-    def product(part, spec_ref):
-        spec_ref[...] = jnp.dot(
-            mix_ref[...], grid_ref[part], preferred_element_type=jnp.float32
-        )
+    def product(part):
+        return jnp.dot(mix_ref[...], grid_ref[part], preferred_element_type=jnp.float32)
 
     def send(part, which):
         target = (cross_hbm, diff_hbm)[which]
@@ -140,14 +173,14 @@
             out_sem.at[part, which],
         )
 
-    specs = (even_ref, odd_ref)
-    product(0, specs[0])
     for part in range(4):
-        if part < 3:
-            product(part + 1, specs[(part + 1) % 2])
-        combine(part, specs[part % 2])
-        for which in range(2):
-            send(part, which).start()
+        combine(part, product(part))
+        if part == 2:
+            for done in range(3):
+                for which in range(2):
+                    send(done, which).start()
+    for which in range(2):
+        send(3, which).start()
     for part in range(4):
         for which in range(2):
             send(part, which).wait()
@@ -202,9 +235,17 @@
     hbm = pl.BlockSpec(memory_space=pl.ANY)
     outgoing = pl.pallas_call(
         send_kernel,
-        out_shape=jax.ShapeDtypeStruct((devices, 2 * doubled + META, LANES), jnp.bfloat16),
-        in_specs=[smem] * 4 + [vmem] * 3,
+        out_shape=jax.ShapeDtypeStruct((devices, doubled + 1, PAIR, LANES), jnp.bfloat16),
+        in_specs=[smem] * 4 + [vmem] + [hbm] * 2,
         out_specs=vmem,
+        scratch_shapes=[
+            pltpu.VMEM(samples.shape, samples.dtype),
+            pltpu.VMEM(weights.shape, weights.dtype),
+            pltpu.VMEM((16, doubled + 1, PAIR, LANES), jnp.bfloat16),
+            pltpu.SemaphoreType.DMA,
+            pltpu.SemaphoreType.DMA((2,)),
+            pltpu.SemaphoreType.DMA((devices // 16,)),
+        ],
     )(
         block_tile[0, 0],
         block_chan[0, 0],
@@ -238,14 +279,12 @@
         scratch_shapes=[
             pltpu.VMEM(inv_cov.shape, jnp.bfloat16),
             pltpu.VMEM((4, channels, 4 * LANES), jnp.bfloat16),
-            pltpu.VMEM((channels, 4 * LANES), jnp.float32),
-            pltpu.VMEM((channels, 4 * LANES), jnp.float32),
             pltpu.VMEM((4, 2, channels, LANES), jnp.float32),
             pltpu.SemaphoreType.DMA,
             pltpu.SemaphoreType.DMA((4, 2)),
         ],
         compiler_params=pltpu.CompilerParams(vmem_limit_bytes=LIMIT * 2**20),
-    )(received, mix)
+    )(received.reshape(-1, LANES), mix)
 
 
 def solution(mesh):

time: 57.3 us -> 55.6 us (0.970)
  waiting for transfers between devices: 27.2 us -> 25.1 us
    all_to_all x1, waiting for transfers between devices: 27.2 us -> 25.1 us  [on_device(): lax.all_to_all(outgoing, AXES, split_axis=0, concat_axis=0, tiled=True)]
  transfers between devices with their start and end apart: 1 -> 1, of which waited for: 1 -> 1; matrix products, arithmetic and copies ran while one was open for 0% -> 0% of each run, Pallas kernels for 10% -> 11%
where the time goes in v4:
time: 55.6 us; the launch traced here: 55.3 us
  waiting for transfers between devices  25.1 us (45%)
  Pallas kernels  18 us (32%)
  starting transfers between devices  11.5 us (21%)
  between operations  0.66 us (1%)
    all_to_all x1, waiting for transfers between devices, on_device(): lax.all_to_all(outgoing, AXES, split_axis=0, concat_axis=0, tiled=True)  25.1 us
    all_to_all x1, starting transfers between devices, on_device(): lax.all_to_all(outgoing, AXES, split_axis=0, concat_axis=0, tiled=True)  11.5 us
    pallas_call x1, Pallas kernels, on_device(): pl.pallas_call(grid_kernel, out_shape=(shape, shape), in_specs=[vmem, hbm...  7.95 us
    pallas_call x1, Pallas kernels, on_device(): pl.pallas_call(mix_kernel, out_shape=jax.ShapeDtypeStruct((SPARE,) + inv_...  5.91 us
    pallas_call x1, Pallas kernels, on_device(): pl.pallas_call(send_kernel, out_shape=jax.ShapeDtypeStruct((devices, doub...  4.15 us
  transfers between devices with their start and end apart: 1, of which 1 were waited for; matrix products, arithmetic and copies ran while one was open for 0% of the time, Pallas kernels for 11%

profile of v4, /device:TPU:1, one launch (start us, length us, event | category | flops | bytes accessed | tf_op | source)
XLA Modules:
  0.0 55.3 jit_solution(18398156742735095505)
XLA Ops:
  0.6 4.1 %shard_map.77 = bf16[128,33,2,128]{3,2,1,0:T(2,128)(2,1)} custom-call(s32[32]{0:T(128)} %bitcast.11, s32[32]{0:T(128)} %bitcast.12, s32[256]{0:T(256)} %owner_ref.1, s32[1]{0:T(128)} %bitcast.2.place_ref, s32[2,128]{1,0:T(2,128)} %bitcast.10, bf16[32,32,128]{2,1,0:T(8,128)(2,1)} %bitcast.9, bf16[32,128,256]{2,1,0:T(8,128)(2,1)} %bitcast.8), custom_call_target="tpu_custom_call" | custom-call | tf_op jit(solution)/shard_map/pallas_call | solution.py:236
  4.8 11.5 %all-to-all-start = ((bf16[128,33,2,128]{3,2,1,0:T(2,128)(2,1)}), bf16[128,33,2,128]{3,2,1,0:T(2,128)(2,1)S(1)}, u32[]{:S(2)}, u32[]{:S(2)}) async-start(bf16[128,33,2,128]{3,2,1,0:T(2,128)(2,1)} %shard_map.77), calls=%async_computation | async-start | bytes 4325376 | tf_op jit(solution)/shard_map/all_to_all | solution.py:258
  16.3 5.9 %shard_map.78.mix_hbm = bf16[8,1024,1024]{2,1,0:T(8,128)(2,1)} custom-call(bf16[1024,1024]{1,0:T(8,128)(2,1)} %cov_ref.1), custom_call_target="tpu_custom_call" | custom-call | flops 2147483648 | bytes 4194304 | tf_op jit(solution)/shard_map/pallas_call | solution.py:259
  22.2 25.1 %all-to-all-done = bf16[128,33,2,128]{3,2,1,0:T(2,128)(2,1)S(1)} async-done(((bf16[128,33,2,128]{3,2,1,0:T(2,128)(2,1)}), bf16[128,33,2,128]{3,2,1,0:T(2,128)(2,1)S(1)}, u32[]{:S(2)}, u32[]{:S(2)}) %all-to-all-start) | async-done | bytes 2162720 | tf_op jit(solution)/shard_map/all_to_all | solution.py:258
  47.3 7.9 %shard_map.79 = (f32[1024,512]{1,0:T(8,128)}, f32[1024,512]{1,0:T(8,128)}) custom-call(bf16[8448,128]{1,0:T(8,128)(2,1)S(1)} %bitcast.7, bf16[8,1024,1024]{2,1,0:T(8,128)(2,1)} %shard_map.78.mix_hbm), custom_call_target="tpu_custom_call" | custom-call | tf_op jit(solution)/shard_map/pallas_call | solution.py:274
Async XLA Ops:
  4.8 42.6 %all-to-all-start = ((bf16[128,33,2,128]{3,2,1,0:T(2,128)(2,1)}), bf16[128,33,2,128]{3,2,1,0:T(2,128)(2,1)S(1)}, u32[]{:S(2)}, u32[]{:S(2)}) async-start(bf16[128,33,2,128]{3,2,1,0:T(2,128)(2,1)} %shard_map.77), calls=%async_computation | async-start | bytes 4325376 | tf_op jit(solution)/shard_map/all_to_all | solution.py:258

commit v5 on v4

--- a/solution.py
+++ b/solution.py
@@ -143,12 +143,17 @@
         d_i = a_i - b_i
         return a_r * b_r + a_i * b_i, d_r * d_r + d_i * d_i
 
-    def combine(part, spec):
-        for index in range(half // 8):
-            row = index * 8
-            cos = [spec[row : row + 8, k * LANES : (k + 1) * LANES] for k in range(4)]
-            sin = [spec[half + row : half + row + 8, k * LANES : (k + 1) * LANES] for k in range(4)]
-            if index == 0:
+    size = half // 2
+
+    def combine(part, block, spec):
+        for index in range(size // 8):
+            local = index * 8
+            row = block * size + local
+            cos = [spec[local : local + 8, k * LANES : (k + 1) * LANES] for k in range(4)]
+            sin = [
+                spec[size + local : size + local + 8, k * LANES : (k + 1) * LANES] for k in range(4)
+            ]
+            if row == 0:
                 for which, power in enumerate(powers(*sin)):
                     out_ref[part, which, half : half + 1, :] = power[:1]
                 sin = [jnp.where(sub > 0, value, 0.0) for value in sin]
@@ -159,11 +164,16 @@
                 out_ref[part, which, row : row + 8, :] = lower[which]
                 mirrored = jnp.take_along_axis(upper[which], flip, axis=0, mode="promise_in_bounds")
                 out_ref[part, which, top - 7 : top, :] = mirrored[1:]
-                if index > 0:
+                if row > 0:
                     out_ref[part, which, top : top + 1, :] = mirrored[:1]
 
-    def product(part):
-        return jnp.dot(mix_ref[...], grid_ref[part], preferred_element_type=jnp.float32)
+    def product(part, block):
+        first = block * size
+        rows = jnp.concatenate(
+            [mix_ref[first : first + size, :], mix_ref[half + first : half + first + size, :]],
+            axis=0,
+        )
+        return jnp.dot(rows, grid_ref[part], preferred_element_type=jnp.float32)
 
     def send(part, which):
         target = (cross_hbm, diff_hbm)[which]
@@ -173,9 +183,14 @@
             out_sem.at[part, which],
         )
 
-    for part in range(4):
-        combine(part, product(part))
-        if part == 2:
+    work = [(part, block) for part in range(4) for block in range(2)]
+    ahead = product(*work[0])
+    for index, (part, block) in enumerate(work):
+        spec = ahead
+        if index + 1 < len(work):
+            ahead = product(*work[index + 1])
+        combine(part, block, spec)
+        if index == 5:
             for done in range(3):
                 for which in range(2):
                     send(done, which).start()

time: 55.6 us -> 55.6 us (level)
  no operation moved by 1% of the time
where the time goes in v5:
time: 55.6 us; the launch traced here: 55.3 us
  waiting for transfers between devices  25.1 us (45%)
  Pallas kernels  18 us (32%)
  starting transfers between devices  11.5 us (21%)
  between operations  0.66 us (1%)
    all_to_all x1, waiting for transfers between devices, on_device(): lax.all_to_all(outgoing, AXES, split_axis=0, concat_axis=0, tiled=True)  25.1 us
    all_to_all x1, starting transfers between devices, on_device(): lax.all_to_all(outgoing, AXES, split_axis=0, concat_axis=0, tiled=True)  11.5 us
    pallas_call x1, Pallas kernels, on_device(): pl.pallas_call(grid_kernel, out_shape=(shape, shape), in_specs=[vmem, hbm...  7.97 us
    pallas_call x1, Pallas kernels, on_device(): pl.pallas_call(mix_kernel, out_shape=jax.ShapeDtypeStruct((SPARE,) + inv_...  5.91 us
    pallas_call x1, Pallas kernels, on_device(): pl.pallas_call(send_kernel, out_shape=jax.ShapeDtypeStruct((devices, doub...  4.15 us
  transfers between devices with their start and end apart: 1, of which 1 were waited for; matrix products, arithmetic and copies ran while one was open for 0% of the time, Pallas kernels for 11%

profile of v5, /device:TPU:1, one launch (start us, length us, event | category | flops | bytes accessed | tf_op | source)
XLA Modules:
  0.0 55.3 jit_solution(16932707026319491009)
XLA Ops:
  0.6 4.1 %shard_map.77 = bf16[128,33,2,128]{3,2,1,0:T(2,128)(2,1)} custom-call(s32[32]{0:T(128)} %bitcast.11, s32[32]{0:T(128)} %bitcast.12, s32[256]{0:T(256)} %owner_ref.1, s32[1]{0:T(128)} %bitcast.2.place_ref, s32[2,128]{1,0:T(2,128)} %bitcast.10, bf16[32,32,128]{2,1,0:T(8,128)(2,1)} %bitcast.9, bf16[32,128,256]{2,1,0:T(8,128)(2,1)} %bitcast.8), custom_call_target="tpu_custom_call" | custom-call | tf_op jit(solution)/shard_map/pallas_call | solution.py:251
  4.8 11.5 %all-to-all-start = ((bf16[128,33,2,128]{3,2,1,0:T(2,128)(2,1)}), bf16[128,33,2,128]{3,2,1,0:T(2,128)(2,1)S(1)}, u32[]{:S(2)}, u32[]{:S(2)}) async-start(bf16[128,33,2,128]{3,2,1,0:T(2,128)(2,1)} %shard_map.77), calls=%async_computation | async-start | bytes 4325376 | tf_op jit(solution)/shard_map/all_to_all | solution.py:273
  16.3 5.9 %shard_map.78.mix_hbm = bf16[8,1024,1024]{2,1,0:T(8,128)(2,1)} custom-call(bf16[1024,1024]{1,0:T(8,128)(2,1)} %cov_ref.1), custom_call_target="tpu_custom_call" | custom-call | flops 2147483648 | bytes 4194304 | tf_op jit(solution)/shard_map/pallas_call | solution.py:274
  22.2 25.1 %all-to-all-done = bf16[128,33,2,128]{3,2,1,0:T(2,128)(2,1)S(1)} async-done(((bf16[128,33,2,128]{3,2,1,0:T(2,128)(2,1)}), bf16[128,33,2,128]{3,2,1,0:T(2,128)(2,1)S(1)}, u32[]{:S(2)}, u32[]{:S(2)}) %all-to-all-start) | async-done | bytes 2162720 | tf_op jit(solution)/shard_map/all_to_all | solution.py:273
  47.3 8.0 %shard_map.79 = (f32[1024,512]{1,0:T(8,128)}, f32[1024,512]{1,0:T(8,128)}) custom-call(bf16[8448,128]{1,0:T(8,128)(2,1)S(1)} %bitcast.7, bf16[8,1024,1024]{2,1,0:T(8,128)(2,1)} %shard_map.78.mix_hbm), custom_call_target="tpu_custom_call" | custom-call | tf_op jit(solution)/shard_map/pallas_call | solution.py:289
Async XLA Ops:
  4.8 42.6 %all-to-all-start = ((bf16[128,33,2,128]{3,2,1,0:T(2,128)(2,1)}), bf16[128,33,2,128]{3,2,1,0:T(2,128)(2,1)S(1)}, u32[]{:S(2)}, u32[]{:S(2)}) async-start(bf16[128,33,2,128]{3,2,1,0:T(2,128)(2,1)} %shard_map.77), calls=%async_computation | async-start | bytes 4325376 | tf_op jit(solution)/shard_map/all_to_all | solution.py:273
